TPU v7x, 32 devices: a whole 2x2x4 slice. The times are simulated.
32 devices in a mesh: dp: 2 (over y), seq: 8 (over z, x), tensor: 2 (over core).
Axes of the slice: x: 2, y: 2, z: 4, core: 2. Of those that a mesh axis runs over, the one named last changes fastest.
Arguments:
- tokens: bfloat16 [4, 8192, 512], P('dp', 'seq'), may hold values from -6 to 6
- segments: int32 [4, 8192], P('dp', 'seq'), may hold values from 0 to 15, never falling along the last dimension, each value on 1 to 5120 neighbouring positions
- keep_mask: int32 [4, 8192], P('dp', 'seq'), may hold values 0 or 1
- cotangent: bfloat16 [4, 8192, 512], P('dp', 'seq'), may hold values from -6 to 6
- ln1_gain: float32 [512], replicated, may hold values from 0.25 to 1.75
- ln1_bias: float32 [512], replicated, may hold values from -1.5 to 1.5
- w_qkv: bfloat16 [3, 512, 512], P(None, None, 'tensor'), may hold values from -0.25 to 0.25
- qv_bias: float32 [2, 512], P(None, 'tensor'), may hold values from -1.5 to 1.5
- w_out: bfloat16 [512, 512], P('tensor'), may hold values from -1.5 to 1.5
- b_out: float32 [512], replicated, may hold values from -1.5 to 1.5
- ln2_gain: float32 [512], replicated, may hold values from 0.25 to 1.75
- ln2_bias: float32 [512], replicated, may hold values from -1.5 to 1.5
- w_fc: bfloat16 [512, 2048], P(None, 'tensor'), may hold values from -0.25 to 0.25
- b_fc: float32 [2048], P('tensor'), may hold values from -1.5 to 1.5
- w_proj: bfloat16 [2048, 512], P('tensor'), may hold values from -0.125 to 0.125
- b_proj: float32 [512], replicated, may hold values from -1.5 to 1.5
Outputs:
- layer_out: bfloat16 [4, 8192, 512], P('dp', 'seq')
- grad_tokens: bfloat16 [4, 8192, 512], P('dp', 'seq')
- grad_ln1_gain: float32 [512], replicated
- grad_ln1_bias: float32 [512], replicated
- grad_w_qkv: float32 [3, 512, 512], P(None, None, 'tensor')
- grad_qv_bias: float32 [2, 512], P(None, 'tensor')
- grad_w_out: float32 [512, 512], P('tensor')
- grad_b_out: float32 [512], replicated
- grad_ln2_gain: float32 [512], replicated
- grad_ln2_bias: float32 [512], replicated
- grad_w_fc: float32 [512, 2048], P(None, 'tensor')
- grad_b_fc: float32 [2048], P('tensor')
- grad_w_proj: float32 [2048, 512], P('tensor')
- grad_b_proj: float32 [512], replicated
Inputs may be any that keep to these rules, and one draw needn't show every extreme that they name: `segments`: in each sequence the document numbers never fall; each document holds 1 to 5120 tokens, and one holds exactly 5120.
All inputs are finite; a program needn't handle non-finite values. No bound on the sum of `keep_mask` on one device may be relied on, other than what follows from the above.
Results may differ from a plain program's by a relative error of at most 0.024.
Values may be sent and summed in bfloat16 or wider, within the bound.
No kernel may reach another device: no remote copies, remote signals or barrier semaphores. Data moves between devices by JAX's collectives and lax.ppermute only.
A program may use at most 512 MiB of HBM per device.

v0:
```python
import jax
import jax.numpy as jnp
from jax import lax
from jax.sharding import PartitionSpec as P

HEAD_DIM = 64
EPSILON = 1e-05
MASKED = -1e30


def layer_norm(rows, gain, offset):
    centred = rows - jnp.mean(rows, -1, keepdims=True)
    rstd = lax.rsqrt(jnp.mean(centred * centred, -1, keepdims=True) + EPSILON)
    normed = centred * rstd
    return (normed * gain + offset, normed, rstd)


def norm_back(grad_norm, normed, rstd, gain):
    scaled = grad_norm * gain
    return rstd * (
        scaled
        - jnp.mean(scaled, -1, keepdims=True)
        - normed * jnp.mean(scaled * normed, -1, keepdims=True)
    )


def gelu_parts(pre_act):
    sigma = jax.nn.sigmoid(1.702 * pre_act)
    return (pre_act * sigma, sigma + 1.702 * pre_act * sigma * (1.0 - sigma))


def visible(query_pos, query_seg, key_pos, key_seg, key_keep):
    allowed = (query_seg[:, None] == key_seg[None, :]) & (key_pos[None, :] <= query_pos[:, None])
    return allowed & ((key_keep[None, :] == 1) | (key_pos[None, :] == query_pos[:, None]))


def on_device(
    tokens,
    segments,
    keep_mask,
    cotangent,
    ln1_gain,
    ln1_bias,
    w_qkv,
    qv_bias,
    w_out,
    b_out,
    ln2_gain,
    ln2_bias,
    w_fc,
    b_fc,
    w_proj,
    b_proj,
):
    sequences, group_rows, width = tokens.shape
    local_width = w_qkv.shape[2]
    heads_here = local_width // HEAD_DIM
    score_scale = HEAD_DIM ** (-0.5)
    seg_all, keep_all = (
        lax.all_gather(segments, "seq", axis=1, tiled=True),
        lax.all_gather(keep_mask, "seq", axis=1, tiled=True),
    )
    full_length = seg_all.shape[1]
    key_block = min(512, full_length)
    block_count = full_length // key_block
    piece_index = lax.axis_index("seq")
    query_pos = piece_index * group_rows + jnp.arange(group_rows, dtype=jnp.int32)
    params = (
        ln1_gain,
        ln1_bias,
        w_qkv,
        qv_bias,
        w_out,
        b_out,
        ln2_gain,
        ln2_bias,
        w_fc,
        b_fc,
        w_proj,
        b_proj,
    )
    sums = [jnp.zeros(p.shape, jnp.float32) for p in params]
    outputs = []
    input_grads = []
    for sequence_index in range(sequences):
        rows = tokens[sequence_index].astype(jnp.float32)
        seg_row = seg_all[sequence_index]
        keep_row = keep_all[sequence_index]
        query_seg = segments[sequence_index]
        normed_one_out, normed_one, rstd_one = layer_norm(rows, ln1_gain, ln1_bias)
        hidden_one = normed_one_out.astype(jnp.bfloat16)
        projected = jnp.einsum("te,ced->ctd", hidden_one, w_qkv, preferred_element_type=jnp.float32)
        queries = (projected[0] + qv_bias[0]).astype(jnp.bfloat16)
        keys = projected[1].astype(jnp.bfloat16)
        values = (projected[2] + qv_bias[1]).astype(jnp.bfloat16)
        query_heads = queries.reshape(group_rows, heads_here, HEAD_DIM)
        best = jnp.full((heads_here, group_rows), MASKED, jnp.float32)
        key_part = lax.all_gather(keys, "seq", axis=0, tiled=True)
        value_part = lax.all_gather(values, "seq", axis=0, tiled=True)
        row_count = key_part.shape[0]
        key_pos = jnp.arange(row_count, dtype=jnp.int32)
        key_seg = seg_row
        key_keep = keep_row
        allowed = visible(query_pos, query_seg, key_pos, key_seg, key_keep)[None]
        scores = (
            jnp.einsum(
                "qhd,khd->hqk",
                query_heads,
                key_part.reshape(row_count, heads_here, HEAD_DIM),
                preferred_element_type=jnp.float32,
            )
            * score_scale
        )
        scores = jnp.where(allowed, scores, MASKED)
        new_best = jnp.maximum(best, jnp.max(scores, -1))
        weights = jnp.where(allowed, jnp.exp(scores - new_best[..., None]), 0.0)
        weight_sum = jnp.sum(weights, -1)
        accum = jnp.einsum(
            "hqk,khd->hqd",
            weights.astype(jnp.bfloat16),
            value_part.reshape(row_count, heads_here, HEAD_DIM),
            preferred_element_type=jnp.float32,
        )
        best, weight_sum, accum = (new_best, weight_sum, accum)
        log_sum = best + jnp.log(weight_sum)
        attn_out = (
            (accum / weight_sum[..., None])
            .transpose(1, 0, 2)
            .reshape(group_rows, local_width)
            .astype(jnp.bfloat16)
        )
        attn_term = jnp.dot(attn_out, w_out, preferred_element_type=jnp.float32)
        middle = (
            rows + lax.psum(attn_term.astype(jnp.bfloat16), "tensor").astype(jnp.float32) + b_out
        )
        normed_two_out, normed_two, rstd_two = layer_norm(middle, ln2_gain, ln2_bias)
        hidden_two = normed_two_out.astype(jnp.bfloat16)
        pre_act = jnp.dot(hidden_two, w_fc, preferred_element_type=jnp.float32) + b_fc
        activated, slope = gelu_parts(pre_act)
        act_low = activated.astype(jnp.bfloat16)
        feed_term = jnp.dot(act_low, w_proj, preferred_element_type=jnp.float32)
        feed = lax.psum(feed_term.astype(jnp.bfloat16), "tensor").astype(jnp.float32) + b_proj
        outputs.append((middle + feed).astype(jnp.bfloat16))
        grad_out = cotangent[sequence_index]
        grad_out_wide = grad_out.astype(jnp.float32)
        sums[11] = sums[11] + jnp.sum(grad_out_wide, 0)
        sums[10] = sums[10] + jnp.einsum(
            "tf,td->fd", act_low, grad_out, preferred_element_type=jnp.float32
        )
        grad_act = jnp.einsum("td,fd->tf", grad_out, w_proj, preferred_element_type=jnp.float32)
        grad_pre = (grad_act * slope).astype(jnp.bfloat16)
        sums[9] = sums[9] + jnp.sum(grad_pre.astype(jnp.float32), 0)
        sums[8] = sums[8] + jnp.einsum(
            "te,tf->ef", hidden_two, grad_pre, preferred_element_type=jnp.float32
        )
        grad_hidden_two = lax.psum(
            jnp.einsum("tf,ef->te", grad_pre, w_fc, preferred_element_type=jnp.float32).astype(
                jnp.bfloat16
            ),
            "tensor",
        ).astype(jnp.float32)
        sums[6] = sums[6] + jnp.sum(grad_hidden_two * normed_two, 0)
        sums[7] = sums[7] + jnp.sum(grad_hidden_two, 0)
        grad_middle = grad_out_wide + norm_back(grad_hidden_two, normed_two, rstd_two, ln2_gain)
        grad_branch = grad_middle.astype(jnp.bfloat16)
        sums[5] = sums[5] + jnp.sum(grad_branch.astype(jnp.float32), 0)
        sums[4] = sums[4] + jnp.einsum(
            "tc,td->cd", attn_out, grad_branch, preferred_element_type=jnp.float32
        )
        grad_mixed = jnp.einsum(
            "td,cd->tc", grad_branch, w_out, preferred_element_type=jnp.float32
        ).astype(jnp.bfloat16)
        grad_heads = grad_mixed.reshape(group_rows, heads_here, HEAD_DIM)
        row_dot = jnp.sum(
            (grad_mixed.astype(jnp.float32) * attn_out.astype(jnp.float32)).reshape(
                group_rows, heads_here, HEAD_DIM
            ),
            -1,
        ).T
        key_use, value_use = (
            lax.all_gather(keys, "seq", axis=0, tiled=True),
            lax.all_gather(values, "seq", axis=0, tiled=True),
        )

        def make_step(key_src, value_src, seg_src, keep_src, pos_base, block_rows):

            def key_step(grad_query_sum, block_index):
                first_row = block_index * block_rows
                key_part = lax.dynamic_slice_in_dim(key_src, first_row, block_rows).reshape(
                    block_rows, heads_here, HEAD_DIM
                )
                value_part = lax.dynamic_slice_in_dim(value_src, first_row, block_rows).reshape(
                    block_rows, heads_here, HEAD_DIM
                )
                key_pos = pos_base + first_row + jnp.arange(block_rows, dtype=jnp.int32)
                key_seg = lax.dynamic_slice_in_dim(seg_src, first_row, block_rows)
                key_keep = lax.dynamic_slice_in_dim(keep_src, first_row, block_rows)
                allowed = visible(query_pos, query_seg, key_pos, key_seg, key_keep)[None]
                scores = (
                    jnp.einsum(
                        "qhd,khd->hqk", query_heads, key_part, preferred_element_type=jnp.float32
                    )
                    * score_scale
                )
                probs = jnp.where(allowed, jnp.exp(scores - log_sum[..., None]), 0.0)
                grad_probs = jnp.einsum(
                    "qhd,khd->hqk", grad_heads, value_part, preferred_element_type=jnp.float32
                )
                grad_scores = (probs * (grad_probs - row_dot[..., None])).astype(jnp.bfloat16)
                grad_query_sum = grad_query_sum + jnp.einsum(
                    "hqk,khd->qhd", grad_scores, key_part, preferred_element_type=jnp.float32
                )
                key_term = jnp.einsum(
                    "hqk,qhd->khd", grad_scores, query_heads, preferred_element_type=jnp.float32
                )
                value_term = jnp.einsum(
                    "hqk,qhd->khd",
                    probs.astype(jnp.bfloat16),
                    grad_heads,
                    preferred_element_type=jnp.float32,
                )
                return (
                    grad_query_sum,
                    (
                        key_term.reshape(block_rows, local_width),
                        value_term.reshape(block_rows, local_width),
                    ),
                )

            return key_step

        query_start = jnp.zeros((group_rows, heads_here, HEAD_DIM), jnp.float32)
        step_fn = make_step(key_use, value_use, seg_row, keep_row, 0, key_block)
        grad_query_sum, (key_terms, value_terms) = lax.scan(
            step_fn, query_start, jnp.arange(block_count, dtype=jnp.int32)
        )
        key_terms = key_terms.reshape(full_length, local_width) * score_scale
        value_terms = value_terms.reshape(full_length, local_width)
        key_grads, value_grads = (
            lax.psum_scatter(
                key_terms.astype(jnp.bfloat16), "seq", scatter_dimension=0, tiled=True
            ).astype(jnp.float32),
            lax.psum_scatter(
                value_terms.astype(jnp.bfloat16), "seq", scatter_dimension=0, tiled=True
            ).astype(jnp.float32),
        )
        grad_queries = (
            (grad_query_sum * score_scale).reshape(group_rows, local_width).astype(jnp.bfloat16)
        )
        value_low = value_grads.astype(jnp.bfloat16)
        stacked = jnp.stack([grad_queries, key_grads.astype(jnp.bfloat16), value_low])
        sums[2] = sums[2] + jnp.einsum(
            "te,ctd->ced", hidden_one, stacked, preferred_element_type=jnp.float32
        )
        sums[3] = sums[3] + jnp.stack(
            [
                jnp.sum(grad_queries.astype(jnp.float32), 0),
                jnp.sum(value_low.astype(jnp.float32), 0),
            ]
        )
        grad_hidden_one = lax.psum(
            jnp.einsum("ctd,ced->te", stacked, w_qkv, preferred_element_type=jnp.float32).astype(
                jnp.bfloat16
            ),
            "tensor",
        ).astype(jnp.float32)
        sums[0] = sums[0] + jnp.sum(grad_hidden_one * normed_one, 0)
        sums[1] = sums[1] + jnp.sum(grad_hidden_one, 0)
        grad_rows = grad_middle + norm_back(grad_hidden_one, normed_one, rstd_one, ln1_gain)
        input_grads.append(grad_rows.astype(jnp.bfloat16))
    totals = (
        lax.psum(sums[0].astype(jnp.bfloat16), ("dp", "seq")).astype(jnp.float32),
        lax.psum(sums[1].astype(jnp.bfloat16), ("dp", "seq")).astype(jnp.float32),
        lax.psum(sums[2].astype(jnp.bfloat16), ("dp", "seq")).astype(jnp.float32),
        lax.psum(sums[3].astype(jnp.bfloat16), ("dp", "seq")).astype(jnp.float32),
        lax.psum(sums[4].astype(jnp.bfloat16), ("dp", "seq")).astype(jnp.float32),
        lax.psum(sums[5].astype(jnp.bfloat16), ("dp", "seq")).astype(jnp.float32),
        lax.psum(sums[6].astype(jnp.bfloat16), ("dp", "seq")).astype(jnp.float32),
        lax.psum(sums[7].astype(jnp.bfloat16), ("dp", "seq")).astype(jnp.float32),
        lax.psum(sums[8].astype(jnp.bfloat16), ("dp", "seq")).astype(jnp.float32),
        lax.psum(sums[9].astype(jnp.bfloat16), ("dp", "seq")).astype(jnp.float32),
        lax.psum(sums[10].astype(jnp.bfloat16), ("dp", "seq")).astype(jnp.float32),
        lax.psum(sums[11].astype(jnp.bfloat16), ("dp", "seq")).astype(jnp.float32),
    )
    return (
        jnp.stack(outputs),
        jnp.stack(input_grads),
        totals[0],
        totals[1],
        totals[2],
        totals[3],
        totals[4],
        totals[5],
        totals[6],
        totals[7],
        totals[8],
        totals[9],
        totals[10],
        totals[11],
    )


def solution(mesh):
    return jax.shard_map(
        on_device,
        mesh=mesh,
        in_specs=(
            P("dp", "seq", None),
            P("dp", "seq"),
            P("dp", "seq"),
            P("dp", "seq", None),
            P(),
            P(),
            P(None, None, "tensor"),
            P(None, "tensor"),
            P("tensor", None),
            P(),
            P(),
            P(),
            P(None, "tensor"),
            P("tensor"),
            P("tensor", None),
            P(),
        ),
        out_specs=(
            P("dp", "seq", None),
            P("dp", "seq", None),
            P(),
            P(),
            P(None, None, "tensor"),
            P(None, "tensor"),
            P("tensor", None),
            P(),
            P(),
            P(),
            P(None, "tensor"),
            P("tensor"),
            P("tensor", None),
            P(),
        ),
        check_vma=False,
    )
```

profile of v0, /device:TPU:0, one launch (start us, length us, event | category | flops | bytes accessed | tf_op | source)
XLA Modules:
  0.0 1566.7 jit_solution(10269686080167025364)
XLA Ops:
  23.1 32.7 %all_gather.22 = s32[2,8192]{1,0:T(2,128)S(1)} all-gather(s32[2,1024]{1,0:T(2,128)S(1)} %copy-done.84), channel_id=1, replica_groups=mesh['dp'=2,'seq'=8,'tensor'=2] {'seq'}, dimensions={1}, use_global_device_ids=true | all-gather | bytes 73728 | tf_op jit(solution)/shard_map/all_gather | solution.py:60
  58.3 31.5 %all_gather.23 = s32[2,8192]{1,0:T(2,128)S(1)} all-gather(s32[2,1024]{1,0:T(2,128)S(1)} %copy-done.89), channel_id=1, replica_groups=mesh['dp'=2,'seq'=8,'tensor'=2] {'seq'}, dimensions={1}, use_global_device_ids=true | all-gather | bytes 73728 | tf_op jit(solution)/shard_map/all_gather | solution.py:61
  92.1 24.5 %fusion.37 = (pred[1024,8192]{1,0:T(8,128)(4,1)}, pred[1024,8192]{1,0:T(8,128)(4,1)}) fusion(s32[8192]{0:T(1024)S(1)} %bitcast.455, s32[1024]{0:T(1024)S(1)} %iota_add_fusion.4, s32[1024]{0:T(1024)S(1)} %bitcast.451, pred[8192]{0:T(1024)(128)(4,1)S(1)} %get-tuple-element.339, pred[8192]{0:T(1024)(128)(4,1)S(1)} %get-tuple-element.338, ...), kind=kLoop, calls=%fused_computation.59 | loop fusion | flops 83886080 | bytes 16871424 | tf_op jit(solution)/shard_map/and | solution.py:34
  116.7 50.0 %fusion.20 = (f32[4,1024]{1,0:T(4,128)S(1)}, f32[4,1024,8192]{2,1,0:T(8,128)}) fusion(pred[1024,8192]{1,0:T(8,128)(4,1)} %get-tuple-element.451, bf16[1024,4,64]{0,2,1:T(8,128)(2,1)S(1)} %get-tuple-element.729, bf16[8192,4,64]{0,2,1:T(8,128)(2,1)} %bitcast.448), kind=kOutput, calls=%fused_computation.42 | convolution fusion | flops 4395626496 | bytes 147341312 | tf_op jit(solution)/shard_map/qhd,khd->hqk/dot_general | solution.py:106
  166.8 50.2 %fusion.21 = (f32[4,1024]{1,0:T(4,128)S(1)}, f32[4,1024,8192]{2,1,0:T(8,128)}) fusion(pred[1024,8192]{1,0:T(8,128)(4,1)} %get-tuple-element.450, bf16[1024,4,64]{0,2,1:T(8,128)(2,1)S(1)} %get-tuple-element.672, bf16[8192,4,64]{0,2,1:T(8,128)(2,1)} %bitcast.445), kind=kOutput, calls=%fused_computation.43 | convolution fusion | flops 4395626496 | bytes 147341312 | tf_op jit(solution)/shard_map/qhd,khd->hqk/dot_general | solution.py:106
  217.6 44.0 %fusion.22 = f32[4,1024]{1,0:T(4,128)S(1)} fusion(f32[4,1024,8192]{2,1,0:T(8,128)} %get-tuple-element.459, f32[4,1024]{1,0:T(4,128)S(1)} %broadcast_maximum_fusion.1, pred[1024,8192]{1,0:T(8,128)(4,1)} %get-tuple-element.451), kind=kLoop, calls=%fused_computation.44 | loop fusion | flops 167768064 | bytes 142639104 | tf_op jit(solution)/shard_map/reduce_sum | solution.py:117
  261.7 51.2 %divide_convert_fusion.1 = bf16[1024,4,64]{0,2,1:T(8,128)(2,1)S(1)} fusion(bf16[8192,4,64]{0,2,1:T(8,128)(2,1)} %bitcast.450, f32[4,1024,8192]{2,1,0:T(8,128)} %get-tuple-element.459, f32[4,1024]{1,0:T(4,128)S(1)} %broadcast_maximum_fusion.1, pred[1024,8192]{1,0:T(8,128)(4,1)} %get-tuple-element.451, f32[1024,4]{0,1:T(4,128)S(1)} %bitcast.460), kind=kOutput, calls=%fused_computation.207 | convolution fusion | flops 4463263744 | bytes 147357696 | tf_op jit(solution)/shard_map/hqk,khd->hqd/dot_general | solution.py:118
  314.3 43.9 %fusion.24 = f32[4,1024]{1,0:T(4,128)S(1)} fusion(f32[4,1024,8192]{2,1,0:T(8,128)} %get-tuple-element.461, f32[4,1024]{1,0:T(4,128)S(1)} %broadcast_maximum_fusion, pred[1024,8192]{1,0:T(8,128)(4,1)} %get-tuple-element.450), kind=kLoop, calls=%fused_computation.46 | loop fusion | flops 167768064 | bytes 142639104 | tf_op jit(solution)/shard_map/reduce_sum | solution.py:117
  358.2 51.0 %divide_convert_fusion = bf16[1024,4,64]{0,2,1:T(8,128)(2,1)} fusion(bf16[8192,4,64]{0,2,1:T(8,128)(2,1)} %bitcast.447, f32[4,1024,8192]{2,1,0:T(8,128)} %get-tuple-element.461, f32[4,1024]{1,0:T(4,128)S(1)} %broadcast_maximum_fusion, pred[1024,8192]{1,0:T(8,128)(4,1)} %get-tuple-element.450, f32[1024,4]{0,1:T(4,128)S(1)} %bitcast.459), kind=kOutput, calls=%fused_computation.205 | convolution fusion | flops 4463263744 | bytes 147357696 | tf_op jit(solution)/shard_map/hqk,khd->hqd/dot_general | solution.py:118
  412.2 21.7 %all-reduce.16.cloned.1.call-done = (bf16[1024,512]{1,0:T(8,128)(2,1)}, bf16[1024,512]{1,0:T(8,128)(2,1)}) async-done(((bf16[1024,512]{1,0:T(8,128)(2,1)}, bf16[1024,512]{1,0:T(8,128)(2,1)}), (bf16[1024,512]{1,0:T(8,128)(2,1)}, bf16[1024,512]{1,0:T(8,128)(2,1)})) %all-reduce.16.cloned.1.call-update) | async-done | bytes 2097168 | tf_op jit(solution)/shard_map/psum | solution.py:134
  439.4 5.0 multiply_convert_fusion.5
  462.7 15.1 all-reduce.14.cloned.1.call-done
  477.8 5.1 fusion.86
  493.0 300.7 %while.30 = (s32[]{:T(128)}, f32[1024,4,64]{0,2,1:T(8,128)S(1)}, f32[16,512,256]{1,2,0:T(8,128)}, bf16[16,512,256]{1,2,0:T(8,128)(2,1)}, s32[16]{0:T(128)S(1)}, ...) while((s32[]{:T(128)}, f32[1024,4,64]{0,2,1:T(8,128)S(1)}, ...), condition=%wide.region_21.22_spmd.clone, body=%wide.region_20.21_spmd.clone.sunk | while | flops 1366820864 | bytes 135865776 | solution.py:234
  793.7 6.9 copy.56
  801.3 6.6 multiply_convert_fusion.1
  808.0 6.3 copy.55
  821.6 302.6 %while.31 = (s32[]{:T(128)}, f32[1024,4,64]{0,2,1:T(8,128)S(1)}, f32[16,512,256]{1,2,0:T(8,128)}, bf16[16,512,256]{1,2,0:T(8,128)(2,1)}, s32[16]{0:T(128)S(1)}, ...) while((s32[]{:T(128)}, f32[1024,4,64]{0,2,1:T(8,128)S(1)}, ...), condition=%wide.region_32.33_spmd.clone, body=%wide.region_31.32_spmd.clone.sunk | while | flops 1366820864 | bytes 135865776 | solution.py:234
  826.9 4.7 fusion.263
  865.0 4.7 fusion.263
  940.8 4.7 fusion.263
  978.7 4.7 fusion.263
  1073.0 4.7 fusion.263
  1124.2 6.8 copy.59
  1131.1 6.6 multiply_convert_fusion
  1137.7 6.4 copy.58
  1170.8 49.7 %reduce-scatter.11.cloned.1.call-done = bf16[1024,256]{1,0:T(8,128)(2,1)} async-done(((bf16[8192,256]{1,0:T(8,128)(2,1)}), bf16[1024,256]{1,0:T(8,128)(2,1)}) %reduce-scatter.11.cloned.1.call-update) | async-done | bytes 524304 | tf_op jit(solution)/shard_map/reduce_scatter | solution.py:243
  1220.4 91.7 %reduce-scatter.9.cloned.1.call-done = bf16[1024,256]{1,0:T(8,128)(2,1)} async-done(((bf16[8192,256]{1,0:T(8,128)(2,1)}), bf16[1024,256]{1,0:T(8,128)(2,1)}) %reduce-scatter.9.cloned.1.call-update) | async-done | bytes 524304 | tf_op jit(solution)/shard_map/reduce_scatter | solution.py:240
  1331.9 134.7 %all-reduce.10.cloned.1.call-done = (bf16[3,512,256]{1,2,0:T(8,128)(2,1)}, bf16[256,512]{1,0:T(8,128)(2,1)}, bf16[512,1024]{1,0:T(8,128)(2,1)}, bf16[1024,512]{1,0:T(8,128)(2,1)}) async-done(((bf16[3,512,256]{1,2,0:T(8,128)(2,1)}, bf16[256,512]{1,0:T(8,128)(2,1)}, bf16[512,1024]{1,0:T(8,128)(2,1)}, bf16[1024,512]{1,0:T(8,128)(2,1)}), (bf16[3,512,256]{1,2,0:T(8,128)(2,1)}, bf16[256,512]{1,0:T(8,128)(2,1)}, ...) | async-done | bytes 3145744 | tf_op jit(solution)/shard_map/psum | solution.py:274
  1474.4 23.3 %all-reduce.12.cloned.1.call-done = (bf16[1024,512]{1,0:T(8,128)(2,1)}, bf16[1024,512]{1,0:T(8,128)(2,1)}, bf16[1024,512]{1,0:T(8,128)(2,1)}, bf16[1024,512]{1,0:T(8,128)(2,1)}) async-done(((bf16[1024,512]{1,0:T(8,128)(2,1)}, bf16[1024,512]{1,0:T(8,128)(2,1)}, bf16[1024,512]{1,0:T(8,128)(2,1)}, bf16[1024,512]{1,0:T(8,128)(2,1)}), (bf16[1024,512]{1,0:T(8,128)(2,1)}, bf16[1024,512]{1,0:T(8,128)(2,1)}, ...) | async-done | bytes 4194320 | tf_op jit(solution)/shard_map/psum | solution.py:142
  1497.7 6.0 fusion.87
  1503.8 42.9 %all-reduce = (bf16[512]{0:T(512)(128)(2,1)S(1)}, bf16[512]{0:T(512)(128)(2,1)S(1)}, bf16[2,256]{1,0:T(2,128)(2,1)S(1)}, bf16[512]{0:T(512)(128)(2,1)S(1)}, bf16...) all-reduce(bf16[512]{0:T(512)(128)(2,1)S(1)} %add_convert_fusion.15, ...), channel_id=1, replica_groups=mesh['dp'=2,'seq'=8,'tensor'=2] {'dp','seq'}, use_global_device_ids=true, to_apply=%region_40.41 | all-reduce | flops 4608 | bytes 18432 | tf_op jit(solution)/shard_map/psum | solution.py:272
  (1108 shorter events, 690.9 us)
Async XLA Ops:
  7.2 430.6 %copy-start = (bf16[512,1024]{1,0:T(8,128)(2,1)S(1)}, bf16[512,1024]{1,0:T(8,128)(2,1)}, u32[]{:S(2)}) copy-start(bf16[512,1024]{1,0:T(8,128)(2,1)} %param.32) | copy-start | bytes 3145732
  7.2 109.5 %all-gather.11.cloned.1.call-start = ((), (), s32[]{:S(2)}) async-start(), calls=%async_computation.10 | async-start | bytes 4718592 | tf_op jit(solution)/shard_map/all_gather | solution.py:98
  14.5 152.3 %all-gather.13.cloned.1.call-start = ((), (), s32[]{:S(2)}) async-start(), calls=%async_computation.11 | async-start | bytes 4718592 | tf_op jit(solution)/shard_map/all_gather | solution.py:98
  19.6 242.0 %all-gather.7.cloned.1.call-start = ((), (), s32[]{:S(2)}) async-start(), calls=%async_computation.4 | async-start | bytes 4718592 | tf_op jit(solution)/shard_map/all_gather | solution.py:99
  22.4 335.8 %all-gather.9.cloned.1.call-start = ((), (), s32[]{:S(2)}) async-start(), calls=%async_computation.5 | async-start | bytes 4718592 | tf_op jit(solution)/shard_map/all_gather | solution.py:99
  23.0 410.8 %all-reduce.16.cloned.1.call-start = ((), (), s32[]{:S(2)}) async-start(), calls=%async_computation.15 | async-start | bytes 4194304 | tf_op jit(solution)/shard_map/psum | solution.py:134
  55.8 36.3 %copy-start.54 = (s32[1,1024]{1,0:T(1,128)}, s32[1,1024]{1,0:T(1,128)S(1)}, u32[]{:S(2)}) copy-start(s32[1,1024]{1,0:T(1,128)S(1)} %get-tuple-element.669) | copy-start | bytes 12292
  55.8 36.3 %copy-start.56 = (s32[1,1024]{1,0:T(1,128)}, s32[1,1024]{1,0:T(1,128)S(1)}, u32[]{:S(2)}) copy-start(s32[1,1024]{1,0:T(1,128)S(1)} %get-tuple-element.726) | copy-start | bytes 12292
  55.8 34.9 %slice-start = ((f32[3,1024,256]{1,2,0:T(8,128)}), f32[1,1024,256]{1,2,0:T(8,128)S(1)}, s32[]{:S(2)}) async-start(f32[3,1024,256]{1,2,0:T(8,128)} %copy-done.36), calls=%async_computation.16 | async-start | bytes 2097152 | tf_op jit(solution)/shard_map/slice | solution.py:93
  58.3 58.4 %copy-start.58 = (s32[1,8192]{1,0:T(1,128)}, s32[1,8192]{1,0:T(1,128)S(1)}, u32[]{:S(2)}) copy-start(s32[1,8192]{1,0:T(1,128)S(1)} %get-tuple-element.444) | copy-start | bytes 98308
  58.3 58.4 %copy-start.59 = (s32[1,8192]{1,0:T(1,128)}, s32[1,8192]{1,0:T(1,128)S(1)}, u32[]{:S(2)}) copy-start(s32[1,8192]{1,0:T(1,128)S(1)} %get-tuple-element.445) | copy-start | bytes 98308
  92.1 24.6 %copy-start.16 = (bf16[1024,4,64]{0,2,1:T(8,128)(2,1)}, bf16[1024,4,64]{0,2,1:T(8,128)(2,1)S(1)}, u32[]{:S(2)}) copy-start(bf16[1024,4,64]{0,2,1:T(8,128)(2,1)S(1)} %get-tuple-element.729) | copy-start | bytes 1572868
  92.1 74.7 %copy-start.14 = (bf16[1024,4,64]{0,2,1:T(8,128)(2,1)}, bf16[1024,4,64]{0,2,1:T(8,128)(2,1)S(1)}, u32[]{:S(2)}) copy-start(bf16[1024,4,64]{0,2,1:T(8,128)(2,1)S(1)} %get-tuple-element.672) | copy-start | bytes 1572868
  166.7 50.3 %copy-start.68 = (f32[4,1024]{1,0:T(4,128)}, f32[4,1024]{1,0:T(4,128)S(1)}, u32[]{:S(2)}) copy-start(f32[4,1024]{1,0:T(4,128)S(1)} %get-tuple-element.458) | copy-start | bytes 49156
  261.6 51.2 %copy-start.64 = (f32[4,1024]{1,0:T(4,128)}, f32[4,1024]{1,0:T(4,128)S(1)}, u32[]{:S(2)}) copy-start(f32[4,1024]{1,0:T(4,128)S(1)} %fusion.22) | copy-start | bytes 49156
  261.7 51.2 %copy-start.37 = (bf16[256,512]{1,0:T(8,128)(2,1)S(1)}, bf16[256,512]{1,0:T(8,128)(2,1)}, u32[]{:S(2)}) copy-start(bf16[256,512]{1,0:T(8,128)(2,1)} %param.28) | copy-start | bytes 786436
  312.8 45.4 %copy-start.32 = (bf16[1024,4,64]{0,2,1:T(8,128)(2,1)}, bf16[1024,4,64]{0,2,1:T(8,128)(2,1)S(1)}, u32[]{:S(2)}) copy-start(bf16[1024,4,64]{0,2,1:T(8,128)(2,1)S(1)} %divide_convert_fusion.1) | copy-start | bytes 1572868
  409.2 24.6 %copy-start.74 = (f32[512]{0:T(512)S(1)}, f32[512]{0:T(512)}, u32[]{:S(2)}) copy-start(f32[512]{0:T(512)} %param.29) | copy-start | bytes 6148
  411.9 65.9 %all-reduce.14.cloned.1.call-start = ((), (), s32[]{:S(2)}) async-start(), calls=%async_computation.14 | async-start | bytes 4194304 | tf_op jit(solution)/shard_map/psum | solution.py:156
  436.3 46.7 %copy-start.72 = (f32[1024]{0:T(1024)}, f32[1024]{0:T(1024)S(1)}, u32[]{:S(2)}) copy-start(f32[1024]{0:T(1024)S(1)} %broadcast_multiply_fusion.10) | copy-start | bytes 12292
  436.3 46.6 %copy-start.70 = (f32[1024]{0:T(1024)}, f32[1024]{0:T(1024)S(1)}, u32[]{:S(2)}) copy-start(f32[1024]{0:T(1024)S(1)} %broadcast_multiply_fusion.8) | copy-start | bytes 12292
  437.8 45.2 %copy-start.80 = (f32[1024]{0:T(1024)}, f32[1024]{0:T(1024)S(1)}, u32[]{:S(2)}) copy-start(f32[1024]{0:T(1024)S(1)} %add_rsqrt_fusion) | copy-start | bytes 12292
  437.8 45.1 %copy-start.82 = (f32[1024]{0:T(1024)}, f32[1024]{0:T(1024)S(1)}, u32[]{:S(2)}) copy-start(f32[1024]{0:T(1024)S(1)} %add_rsqrt_fusion.2) | copy-start | bytes 12292
  455.1 711.9 %reduce-scatter.7.cloned.1.call-start = ((), (), s32[]{:S(2)}) async-start(), calls=%async_computation.7 | async-start | bytes 4718592 | tf_op jit(solution)/shard_map/reduce_scatter | solution.py:243
  800.6 366.4 %reduce-scatter.5.cloned.1.call-start = ((), (), s32[]{:S(2)}) async-start(), calls=%async_computation.6 | async-start | bytes 4718592 | tf_op jit(solution)/shard_map/reduce_scatter | solution.py:240
  817.2 403.2 %reduce-scatter.11.cloned.1.call-start = ((), (), s32[]{:S(2)}) async-start(), calls=%async_computation.9 | async-start | bytes 4718592 | tf_op jit(solution)/shard_map/reduce_scatter | solution.py:243
  1131.1 181.1 %reduce-scatter.9.cloned.1.call-start = ((), (), s32[]{:S(2)}) async-start(), calls=%async_computation.8 | async-start | bytes 4718592 | tf_op jit(solution)/shard_map/reduce_scatter | solution.py:240
  1144.1 322.5 %all-reduce.10.cloned.1.call-start = ((), (), s32[]{:S(2)}) async-start(), calls=%async_computation.12 | async-start | bytes 6291456 | tf_op jit(solution)/shard_map/psum | solution.py:274
  1167.0 145.2 %copy-start.61 = (f32[1024]{0:T(1024)S(1)}, f32[1024]{0:T(1024)}, u32[]{:S(2)}) copy-start(f32[1024]{0:T(1024)} %copy-done.60) | copy-start | bytes 12292
  1167.0 145.1 %copy-start.79 = (f32[1024]{0:T(1024)S(1)}, f32[1024]{0:T(1024)}, u32[]{:S(2)}) copy-start(f32[1024]{0:T(1024)} %copy-done.78) | copy-start | bytes 12292
  1316.2 181.5 %all-reduce.12.cloned.1.call-start = ((), (), s32[]{:S(2)}) async-start(), calls=%async_computation.13 | async-start | bytes 8388608 | tf_op jit(solution)/shard_map/psum | solution.py:142
  1472.8 24.9 %copy-start.98 = (f32[512]{0:T(512)S(1)}, f32[512]{0:T(512)}, u32[]{:S(2)}) copy-start(f32[512]{0:T(512)} %param.35) | copy-start | bytes 6148
  (248 other events, 976.0 us)
Sparse Core Ops, SparseCore 0:
  14.6 77.6 all-gather.10
  95.1 71.6 all-gather.12
  169.6 71.6 all-gather.6
  243.8 71.6 all-gather.8
  412.0 21.7 all-reduce.15
  455.3 22.4 all-reduce.13
  800.7 89.2 reduce-scatter.6
  894.1 87.8 reduce-scatter.4
  1131.2 89.2 reduce-scatter.10
  1224.3 87.7 reduce-scatter.8
  1318.7 147.7 all-reduce.9
  1470.0 27.6 all-reduce.11
where the time goes:
time: 1570 us
  matrix products  660 us (42%)
  waiting for transfers between devices  337 us (21%)
  local copies, waits for them, and re-layouts  215 us (14%)
  other arithmetic  207 us (13%)
  blocking collectives  107 us (7%)
  loops' own time  23.1 us (1%)
  between operations  15.8 us (1%)
    dot_general x32, matrix products, key_step(): jnp.einsum('qhd,khd->hqk', grad_heads, value_part, preferred_element_type...  148 us
    psum x1, waiting for transfers between devices, on_device(): lax.psum(sums[2].astype(jnp.bfloat16), ('dp', 'seq')).astype(jnp.float32)  135 us
    dot_general x32, matrix products, key_step(): jnp.einsum('hqk,khd->qhd', grad_scores, key_part, preferred_element_type=...  105 us
    dot_general x2, matrix products, on_device(): jnp.einsum('hqk,khd->hqd', weights.astype(jnp.bfloat16), value_part.resha...  102 us
    dot_general x2, matrix products, on_device(): jnp.einsum('qhd,khd->hqk', query_heads, key_part.reshape(row_count, heads...  100 us
    reduce_scatter x2, waiting for transfers between devices, on_device(): lax.psum_scatter(key_terms.astype(jnp.bfloat16), 'seq', scatter_dimension...  91.7 us
    reduce_sum x2, other arithmetic, on_device(): weight_sum = jnp.sum(weights, -1)  87.9 us
    dot_general x32, matrix products, key_step(): jnp.einsum('hqk,qhd->khd', probs.astype(jnp.bfloat16), grad_heads, prefer...  58.4 us
  transfers between devices with their start and end apart: 12, of which 7 were waited for; matrix products, arithmetic and copies ran while one was open for 41% of the time, Pallas kernels for 0%

commit v1 on v0

--- a/solution.py
+++ b/solution.py
@@ -271,7 +271,9 @@
     totals = (
         lax.psum(sums[0].astype(jnp.bfloat16), ("dp", "seq")).astype(jnp.float32),
         lax.psum(sums[1].astype(jnp.bfloat16), ("dp", "seq")).astype(jnp.float32),
-        lax.psum(sums[2].astype(jnp.bfloat16), ("dp", "seq")).astype(jnp.float32),
+        lax.psum(lax.psum(sums[2].astype(jnp.bfloat16), axis_name="seq"), axis_name="dp").astype(
+            jnp.float32
+        ),
         lax.psum(sums[3].astype(jnp.bfloat16), ("dp", "seq")).astype(jnp.float32),
         lax.psum(sums[4].astype(jnp.bfloat16), ("dp", "seq")).astype(jnp.float32),
         lax.psum(sums[5].astype(jnp.bfloat16), ("dp", "seq")).astype(jnp.float32),

time: 1570 us -> 1670 us (1.064)
  waiting for transfers between devices: 337 us -> 434 us
    psum x1 -> x3, waiting for transfers between devices: 135 us -> 220 us  [the longest x1 127 us: on_device(): lax.psum(sums[4].astype(jnp.bfloat16), ('dp', 'seq')).astype(jnp.float32)]
  transfers between devices with their start and end apart: 12 -> 14, of which waited for: 7 -> 9; matrix products, arithmetic and copies ran while one was open for 41% -> 39% of each run, Pallas kernels for 0% -> 0%
where the time goes in v1:
time: 1670 us
  matrix products  664 us (40%)
  waiting for transfers between devices  434 us (26%)
  local copies, waits for them, and re-layouts  213 us (13%)
  other arithmetic  206 us (12%)
  blocking collectives  107 us (6%)
  loops' own time  23.1 us (1%)
    dot_general x32, matrix products, key_step(): jnp.einsum('qhd,khd->hqk', grad_heads, value_part, preferred_element_type...  148 us
    psum x1, waiting for transfers between devices, on_device(): lax.psum(sums[4].astype(jnp.bfloat16), ('dp', 'seq')).astype(jnp.float32)  127 us
    dot_general x32, matrix products, key_step(): jnp.einsum('hqk,khd->qhd', grad_scores, key_part, preferred_element_type=...  105 us
    dot_general x2, matrix products, on_device(): jnp.einsum('hqk,khd->hqd', weights.astype(jnp.bfloat16), value_part.resha...  102 us
    dot_general x2, matrix products, on_device(): jnp.einsum('qhd,khd->hqk', query_heads, key_part.reshape(row_count, heads...  100 us
    reduce_scatter x2, waiting for transfers between devices, on_device(): lax.psum_scatter(key_terms.astype(jnp.bfloat16), 'seq', scatter_dimension...  91.7 us
    reduce_sum x2, other arithmetic, on_device(): weight_sum = jnp.sum(weights, -1)  87.9 us
    psum x1, waiting for transfers between devices, on_device(): lax.psum(sums[2].astype(jnp.bfloat16), axis_name='seq')  62.6 us
  transfers between devices with their start and end apart: 14, of which 9 were waited for; matrix products, arithmetic and copies ran while one was open for 39% of the time, Pallas kernels for 0%

profile of v1, /device:TPU:0, one launch (start us, length us, event | category | flops | bytes accessed | tf_op | source)
XLA Modules:
  0.0 1665.3 jit_solution(5126285307777044638)
XLA Ops:
  23.1 32.7 %all_gather.22 = s32[2,8192]{1,0:T(2,128)S(1)} all-gather(s32[2,1024]{1,0:T(2,128)S(1)} %copy-done.85), channel_id=1, replica_groups=mesh['dp'=2,'seq'=8,'tensor'=2] {'seq'}, dimensions={1}, use_global_device_ids=true | all-gather | bytes 73728 | tf_op jit(solution)/shard_map/all_gather | solution.py:60
  58.3 31.4 %all_gather.23 = s32[2,8192]{1,0:T(2,128)S(1)} all-gather(s32[2,1024]{1,0:T(2,128)S(1)} %copy-done.90), channel_id=1, replica_groups=mesh['dp'=2,'seq'=8,'tensor'=2] {'seq'}, dimensions={1}, use_global_device_ids=true | all-gather | bytes 73728 | tf_op jit(solution)/shard_map/all_gather | solution.py:61
  92.1 24.5 %fusion.37 = (pred[1024,8192]{1,0:T(8,128)(4,1)}, pred[1024,8192]{1,0:T(8,128)(4,1)}) fusion(s32[8192]{0:T(1024)S(1)} %bitcast.455, s32[1024]{0:T(1024)S(1)} %iota_add_fusion.4, s32[1024]{0:T(1024)S(1)} %bitcast.451, pred[8192]{0:T(1024)(128)(4,1)S(1)} %get-tuple-element.339, pred[8192]{0:T(1024)(128)(4,1)S(1)} %get-tuple-element.338, ...), kind=kLoop, calls=%fused_computation.59 | loop fusion | flops 83886080 | bytes 16871424 | tf_op jit(solution)/shard_map/and | solution.py:34
  116.7 50.0 %fusion.20 = (f32[4,1024]{1,0:T(4,128)S(1)}, f32[4,1024,8192]{2,1,0:T(8,128)}) fusion(pred[1024,8192]{1,0:T(8,128)(4,1)} %get-tuple-element.450, bf16[1024,4,64]{0,2,1:T(8,128)(2,1)S(1)} %get-tuple-element.728, bf16[8192,4,64]{0,2,1:T(8,128)(2,1)} %bitcast.448), kind=kOutput, calls=%fused_computation.42 | convolution fusion | flops 4395626496 | bytes 147341312 | tf_op jit(solution)/shard_map/qhd,khd->hqk/dot_general | solution.py:106
  166.8 50.2 %fusion.21 = (f32[4,1024]{1,0:T(4,128)S(1)}, f32[4,1024,8192]{2,1,0:T(8,128)}) fusion(pred[1024,8192]{1,0:T(8,128)(4,1)} %get-tuple-element.449, bf16[1024,4,64]{0,2,1:T(8,128)(2,1)S(1)} %get-tuple-element.671, bf16[8192,4,64]{0,2,1:T(8,128)(2,1)} %bitcast.445), kind=kOutput, calls=%fused_computation.43 | convolution fusion | flops 4395626496 | bytes 147341312 | tf_op jit(solution)/shard_map/qhd,khd->hqk/dot_general | solution.py:106
  217.6 44.0 %fusion.22 = f32[4,1024]{1,0:T(4,128)S(1)} fusion(f32[4,1024,8192]{2,1,0:T(8,128)} %get-tuple-element.458, f32[4,1024]{1,0:T(4,128)S(1)} %broadcast_maximum_fusion.1, pred[1024,8192]{1,0:T(8,128)(4,1)} %get-tuple-element.450), kind=kLoop, calls=%fused_computation.44 | loop fusion | flops 167768064 | bytes 142639104 | tf_op jit(solution)/shard_map/reduce_sum | solution.py:117
  261.7 51.2 %divide_convert_fusion.1 = bf16[1024,4,64]{0,2,1:T(8,128)(2,1)S(1)} fusion(bf16[8192,4,64]{0,2,1:T(8,128)(2,1)} %bitcast.450, f32[4,1024,8192]{2,1,0:T(8,128)} %get-tuple-element.458, f32[4,1024]{1,0:T(4,128)S(1)} %broadcast_maximum_fusion.1, pred[1024,8192]{1,0:T(8,128)(4,1)} %get-tuple-element.450, f32[1024,4]{0,1:T(4,128)S(1)} %bitcast.460), kind=kOutput, calls=%fused_computation.207 | convolution fusion | flops 4463263744 | bytes 147357696 | tf_op jit(solution)/shard_map/hqk,khd->hqd/dot_general | solution.py:118
  314.3 43.9 %fusion.24 = f32[4,1024]{1,0:T(4,128)S(1)} fusion(f32[4,1024,8192]{2,1,0:T(8,128)} %get-tuple-element.460, f32[4,1024]{1,0:T(4,128)S(1)} %broadcast_maximum_fusion, pred[1024,8192]{1,0:T(8,128)(4,1)} %get-tuple-element.449), kind=kLoop, calls=%fused_computation.46 | loop fusion | flops 167768064 | bytes 142639104 | tf_op jit(solution)/shard_map/reduce_sum | solution.py:117
  358.2 51.0 %divide_convert_fusion = bf16[1024,4,64]{0,2,1:T(8,128)(2,1)} fusion(bf16[8192,4,64]{0,2,1:T(8,128)(2,1)} %bitcast.447, f32[4,1024,8192]{2,1,0:T(8,128)} %get-tuple-element.460, f32[4,1024]{1,0:T(4,128)S(1)} %broadcast_maximum_fusion, pred[1024,8192]{1,0:T(8,128)(4,1)} %get-tuple-element.449, f32[1024,4]{0,1:T(4,128)S(1)} %bitcast.459), kind=kOutput, calls=%fused_computation.205 | convolution fusion | flops 4463263744 | bytes 147357696 | tf_op jit(solution)/shard_map/hqk,khd->hqd/dot_general | solution.py:118
  412.1 21.7 %all-reduce.22.cloned.1.call-done = (bf16[1024,512]{1,0:T(8,128)(2,1)}, bf16[1024,512]{1,0:T(8,128)(2,1)}) async-done(((bf16[1024,512]{1,0:T(8,128)(2,1)}, bf16[1024,512]{1,0:T(8,128)(2,1)}), (bf16[1024,512]{1,0:T(8,128)(2,1)}, bf16[1024,512]{1,0:T(8,128)(2,1)})) %all-reduce.22.cloned.1.call-update) | async-done | bytes 2097168 | tf_op jit(solution)/shard_map/psum | solution.py:134
  439.4 5.0 multiply_convert_fusion.5
  462.6 15.1 all-reduce.20.cloned.1.call-done
  477.7 5.1 fusion.86
  493.0 299.9 %while.30 = (s32[]{:T(128)}, f32[1024,4,64]{0,2,1:T(8,128)S(1)}, f32[16,512,256]{1,2,0:T(8,128)}, bf16[16,512,256]{1,2,0:T(8,128)(2,1)}, s32[16]{0:T(128)S(1)}, ...) while((s32[]{:T(128)}, f32[1024,4,64]{0,2,1:T(8,128)S(1)}, ...), condition=%wide.region_21.22_spmd.clone, body=%wide.region_20.21_spmd.clone.sunk | while | flops 1366820864 | bytes 135865776 | solution.py:234
  792.9 6.8 copy.56
  800.5 6.6 multiply_convert_fusion.1
  807.1 6.3 copy.55
  820.7 302.4 %while.31 = (s32[]{:T(128)}, f32[1024,4,64]{0,2,1:T(8,128)S(1)}, f32[16,512,256]{1,2,0:T(8,128)}, bf16[16,512,256]{1,2,0:T(8,128)(2,1)}, s32[16]{0:T(128)S(1)}, ...) while((s32[]{:T(128)}, f32[1024,4,64]{0,2,1:T(8,128)S(1)}, ...), condition=%wide.region_32.33_spmd.clone, body=%wide.region_31.32_spmd.clone.sunk | while | flops 1366820864 | bytes 135865776 | solution.py:234
  1090.8 4.7 fusion.263
  1123.2 6.8 copy.59
  1130.0 6.5 multiply_convert_fusion
  1136.6 6.4 copy.58
  1143.3 4.7 fusion.110
  1163.5 55.8 %reduce-scatter.11.cloned.1.call-done = bf16[1024,256]{1,0:T(8,128)(2,1)} async-done(((bf16[8192,256]{1,0:T(8,128)(2,1)}), bf16[1024,256]{1,0:T(8,128)(2,1)}) %reduce-scatter.11.cloned.1.call-update) | async-done | bytes 524304 | tf_op jit(solution)/shard_map/reduce_scatter | solution.py:243
  1219.4 91.7 %reduce-scatter.9.cloned.1.call-done = bf16[1024,256]{1,0:T(8,128)(2,1)} async-done(((bf16[8192,256]{1,0:T(8,128)(2,1)}), bf16[1024,256]{1,0:T(8,128)(2,1)}) %reduce-scatter.9.cloned.1.call-update) | async-done | bytes 524304 | tf_op jit(solution)/shard_map/reduce_scatter | solution.py:240
  1315.3 4.9 add_convert_fusion
  1327.2 62.6 %all-reduce.12.cloned.1.call-done = bf16[3,512,256]{1,2,0:T(8,128)(2,1)} async-done(((bf16[3,512,256]{1,2,0:T(8,128)(2,1)}), bf16[3,512,256]{1,2,0:T(8,128)(2,1)}) %all-reduce.12.cloned.1.call-update) | async-done | bytes 786448 | tf_op jit(solution)/shard_map/psum | solution.py:274
  1400.9 127.4 %all-reduce.16.cloned.1.call-done = (bf16[256,512]{1,0:T(8,128)(2,1)}, bf16[512,1024]{1,0:T(8,128)(2,1)}, bf16[1024,512]{1,0:T(8,128)(2,1)}) async-done(((bf16[256,512]{1,0:T(8,128)(2,1)}, bf16[512,1024]{1,0:T(8,128)(2,1)}, bf16[1024,512]{1,0:T(8,128)(2,1)}), (bf16[256,512]{1,0:T(8,128)(2,1)}, bf16[512,1024]{1,0:T(8,128)(2,1)}, bf16[1024,512]{1,0:T(8,128)(2,1)})) %all-reduce.16.cloned.1.call-update) | async-done | bytes 2359312 | tf_op jit(solution)/shard_map/psum | solution.py:278
  1534.9 29.6 %all-reduce.14.cloned.1.call-done = bf16[3,512,256]{1,2,0:T(8,128)(2,1)} async-done(((bf16[3,512,256]{1,2,0:T(8,128)(2,1)}), bf16[3,512,256]{1,2,0:T(8,128)(2,1)}) %all-reduce.14.cloned.1.call-update) | async-done | bytes 786448 | tf_op jit(solution)/shard_map/psum | solution.py:274
  1567.0 29.6 %all-reduce.18.cloned.1.call-done = (bf16[1024,512]{1,0:T(8,128)(2,1)}, bf16[1024,512]{1,0:T(8,128)(2,1)}, bf16[1024,512]{1,0:T(8,128)(2,1)}, bf16[1024,512]{1,0:T(8,128)(2,1)}) async-done(((bf16[1024,512]{1,0:T(8,128)(2,1)}, bf16[1024,512]{1,0:T(8,128)(2,1)}, bf16[1024,512]{1,0:T(8,128)(2,1)}, bf16[1024,512]{1,0:T(8,128)(2,1)}), (bf16[1024,512]{1,0:T(8,128)(2,1)}, bf16[1024,512]{1,0:T(8,128)(2,1)}, ...) | async-done | bytes 4194320 | tf_op jit(solution)/shard_map/psum | solution.py:142
  1596.7 5.9 fusion.87
  1602.7 42.9 %all-reduce = (bf16[512]{0:T(512)(128)(2,1)S(1)}, bf16[512]{0:T(512)(128)(2,1)S(1)}, bf16[2,256]{1,0:T(2,128)(2,1)S(1)}, bf16[512]{0:T(512)(128)(2,1)S(1)}, bf16...) all-reduce(bf16[512]{0:T(512)(128)(2,1)S(1)} %add_convert_fusion.15, ...), channel_id=1, replica_groups=mesh['dp'=2,'seq'=8,'tensor'=2] {'dp','seq'}, use_global_device_ids=true, to_apply=%region_40.41 | all-reduce | flops 4608 | bytes 18432 | tf_op jit(solution)/shard_map/psum | solution.py:272
  (1110 shorter events, 701.5 us)
Async XLA Ops:
  7.2 430.6 %copy-start = (bf16[512,1024]{1,0:T(8,128)(2,1)S(1)}, bf16[512,1024]{1,0:T(8,128)(2,1)}, u32[]{:S(2)}) copy-start(bf16[512,1024]{1,0:T(8,128)(2,1)} %param.32) | copy-start | bytes 3145732
  7.2 109.5 %all-gather.11.cloned.1.call-start = ((), (), s32[]{:S(2)}) async-start(), calls=%async_computation.12 | async-start | bytes 4718592 | tf_op jit(solution)/shard_map/all_gather | solution.py:98
  14.5 152.3 %all-gather.13.cloned.1.call-start = ((), (), s32[]{:S(2)}) async-start(), calls=%async_computation.13 | async-start | bytes 4718592 | tf_op jit(solution)/shard_map/all_gather | solution.py:98
  19.6 242.0 %all-gather.7.cloned.1.call-start = ((), (), s32[]{:S(2)}) async-start(), calls=%async_computation.4 | async-start | bytes 4718592 | tf_op jit(solution)/shard_map/all_gather | solution.py:99
  22.4 335.8 %all-gather.9.cloned.1.call-start = ((), (), s32[]{:S(2)}) async-start(), calls=%async_computation.5 | async-start | bytes 4718592 | tf_op jit(solution)/shard_map/all_gather | solution.py:99
  23.0 410.8 %all-reduce.22.cloned.1.call-start = ((), (), s32[]{:S(2)}) async-start(), calls=%async_computation.17 | async-start | bytes 4194304 | tf_op jit(solution)/shard_map/psum | solution.py:134
  55.8 36.3 %copy-start.55 = (s32[1,1024]{1,0:T(1,128)}, s32[1,1024]{1,0:T(1,128)S(1)}, u32[]{:S(2)}) copy-start(s32[1,1024]{1,0:T(1,128)S(1)} %get-tuple-element.668) | copy-start | bytes 12292
  55.8 36.3 %copy-start.57 = (s32[1,1024]{1,0:T(1,128)}, s32[1,1024]{1,0:T(1,128)S(1)}, u32[]{:S(2)}) copy-start(s32[1,1024]{1,0:T(1,128)S(1)} %get-tuple-element.725) | copy-start | bytes 12292
  55.8 34.9 %slice-start = ((f32[3,1024,256]{1,2,0:T(8,128)}), f32[1,1024,256]{1,2,0:T(8,128)S(1)}, s32[]{:S(2)}) async-start(f32[3,1024,256]{1,2,0:T(8,128)} %copy-done.36), calls=%async_computation.18 | async-start | bytes 2097152 | tf_op jit(solution)/shard_map/slice | solution.py:93
  58.3 58.4 %copy-start.59 = (s32[1,8192]{1,0:T(1,128)}, s32[1,8192]{1,0:T(1,128)S(1)}, u32[]{:S(2)}) copy-start(s32[1,8192]{1,0:T(1,128)S(1)} %get-tuple-element.443) | copy-start | bytes 98308
  58.3 58.4 %copy-start.60 = (s32[1,8192]{1,0:T(1,128)}, s32[1,8192]{1,0:T(1,128)S(1)}, u32[]{:S(2)}) copy-start(s32[1,8192]{1,0:T(1,128)S(1)} %get-tuple-element.444) | copy-start | bytes 98308
  92.1 74.7 %copy-start.14 = (bf16[1024,4,64]{0,2,1:T(8,128)(2,1)}, bf16[1024,4,64]{0,2,1:T(8,128)(2,1)S(1)}, u32[]{:S(2)}) copy-start(bf16[1024,4,64]{0,2,1:T(8,128)(2,1)S(1)} %get-tuple-element.671) | copy-start | bytes 1572868
  166.7 50.3 %copy-start.69 = (f32[4,1024]{1,0:T(4,128)}, f32[4,1024]{1,0:T(4,128)S(1)}, u32[]{:S(2)}) copy-start(f32[4,1024]{1,0:T(4,128)S(1)} %get-tuple-element.457) | copy-start | bytes 49156
  261.6 51.2 %copy-start.65 = (f32[4,1024]{1,0:T(4,128)}, f32[4,1024]{1,0:T(4,128)S(1)}, u32[]{:S(2)}) copy-start(f32[4,1024]{1,0:T(4,128)S(1)} %fusion.22) | copy-start | bytes 49156
  261.7 51.2 %copy-start.37 = (bf16[256,512]{1,0:T(8,128)(2,1)S(1)}, bf16[256,512]{1,0:T(8,128)(2,1)}, u32[]{:S(2)}) copy-start(bf16[256,512]{1,0:T(8,128)(2,1)} %param.28) | copy-start | bytes 786436
  312.8 45.4 %copy-start.31 = (bf16[1024,4,64]{0,2,1:T(8,128)(2,1)}, bf16[1024,4,64]{0,2,1:T(8,128)(2,1)S(1)}, u32[]{:S(2)}) copy-start(bf16[1024,4,64]{0,2,1:T(8,128)(2,1)S(1)} %divide_convert_fusion.1) | copy-start | bytes 1572868
  411.9 65.9 %all-reduce.20.cloned.1.call-start = ((), (), s32[]{:S(2)}) async-start(), calls=%async_computation.16 | async-start | bytes 4194304 | tf_op jit(solution)/shard_map/psum | solution.py:156
  436.3 46.6 %copy-start.73 = (f32[1024]{0:T(1024)}, f32[1024]{0:T(1024)S(1)}, u32[]{:S(2)}) copy-start(f32[1024]{0:T(1024)S(1)} %broadcast_multiply_fusion.10) | copy-start | bytes 12292
  436.3 46.6 %copy-start.71 = (f32[1024]{0:T(1024)}, f32[1024]{0:T(1024)S(1)}, u32[]{:S(2)}) copy-start(f32[1024]{0:T(1024)S(1)} %broadcast_multiply_fusion.8) | copy-start | bytes 12292
  437.8 45.2 %copy-start.81 = (f32[1024]{0:T(1024)}, f32[1024]{0:T(1024)S(1)}, u32[]{:S(2)}) copy-start(f32[1024]{0:T(1024)S(1)} %add_rsqrt_fusion) | copy-start | bytes 12292
  437.8 45.1 %copy-start.83 = (f32[1024]{0:T(1024)}, f32[1024]{0:T(1024)S(1)}, u32[]{:S(2)}) copy-start(f32[1024]{0:T(1024)S(1)} %add_rsqrt_fusion.2) | copy-start | bytes 12292
  455.1 704.6 %reduce-scatter.7.cloned.1.call-start = ((), (), s32[]{:S(2)}) async-start(), calls=%async_computation.7 | async-start | bytes 4718592 | tf_op jit(solution)/shard_map/reduce_scatter | solution.py:243
  799.8 360.0 %reduce-scatter.5.cloned.1.call-start = ((), (), s32[]{:S(2)}) async-start(), calls=%async_computation.6 | async-start | bytes 4718592 | tf_op jit(solution)/shard_map/reduce_scatter | solution.py:240
  816.3 403.1 %reduce-scatter.11.cloned.1.call-start = ((), (), s32[]{:S(2)}) async-start(), calls=%async_computation.9 | async-start | bytes 4718592 | tf_op jit(solution)/shard_map/reduce_scatter | solution.py:243
  1130.0 181.1 %reduce-scatter.9.cloned.1.call-start = ((), (), s32[]{:S(2)}) async-start(), calls=%async_computation.8 | async-start | bytes 4718592 | tf_op jit(solution)/shard_map/reduce_scatter | solution.py:240
  1143.0 246.8 %all-reduce.12.cloned.1.call-start = ((), (), s32[]{:S(2)}) async-start(), calls=%async_computation.10 | async-start | bytes 1572864 | tf_op jit(solution)/shard_map/psum | solution.py:274
  1159.8 151.3 %copy-start.62 = (f32[1024]{0:T(1024)S(1)}, f32[1024]{0:T(1024)}, u32[]{:S(2)}) copy-start(f32[1024]{0:T(1024)} %copy-done.61) | copy-start | bytes 12292
  1159.8 151.3 %copy-start.80 = (f32[1024]{0:T(1024)S(1)}, f32[1024]{0:T(1024)}, u32[]{:S(2)}) copy-start(f32[1024]{0:T(1024)} %copy-done.79) | copy-start | bytes 12292
  1315.2 213.1 %all-reduce.16.cloned.1.call-start = ((), (), s32[]{:S(2)}) async-start(), calls=%async_computation.14 | async-start | bytes 4718592 | tf_op jit(solution)/shard_map/psum | solution.py:278
  1323.1 241.4 %all-reduce.14.cloned.1.call-start = ((), (), s32[]{:S(2)}) async-start(), calls=%async_computation.11 | async-start | bytes 1572864 | tf_op jit(solution)/shard_map/psum | solution.py:274
  1389.8 206.8 %all-reduce.18.cloned.1.call-start = ((), (), s32[]{:S(2)}) async-start(), calls=%async_computation.15 | async-start | bytes 8388608 | tf_op jit(solution)/shard_map/psum | solution.py:142
  1534.6 62.1 %copy-start.99 = (f32[512]{0:T(512)S(1)}, f32[512]{0:T(512)}, u32[]{:S(2)}) copy-start(f32[512]{0:T(512)} %param.35) | copy-start | bytes 6148
  (248 other events, 1065.7 us)
Sparse Core Ops, SparseCore 0:
  14.6 77.6 all-gather.10
  95.1 71.6 all-gather.12
  169.5 71.6 all-gather.6
  243.8 71.6 all-gather.8
  412.0 21.7 all-reduce.21
  455.2 22.4 all-reduce.19
  799.9 89.0 reduce-scatter.6
  893.0 87.8 reduce-scatter.4
  1130.1 89.2 reduce-scatter.10
  1223.3 87.7 reduce-scatter.8
  1315.3 74.4 all-reduce.11
  1397.2 130.9 all-reduce.15
  1530.5 33.8 all-reduce.13
  1567.9 28.7 all-reduce.17
